TPU v7x, 512 devices: a whole 4x8x8 slice. The times are simulated.
512 devices in a mesh: band: 8 (over z), facet: 64 (over x, y, core).
Axes of the slice: x: 4, y: 8, z: 8, core: 2. Of those that a mesh axis runs over, the one named last changes fastest.
Arguments:
- facets: bfloat16 [8, 64, 2, 128, 4096], P('band', 'facet'), may hold values from -6 to 6
- col_window: float32 [4096], replicated, may hold values from 0.25 to 1
- slot_of_subgrid: int32 [96], replicated, may hold values from 0 to 127, as said below
- block_slot: int32 [8, 64, 4], P('band', 'facet'), may hold values from 0 to 1
- block_band: int32 [8, 64, 4], P('band', 'facet'), may hold values from 0 to 6
- block_offset: int32 [8, 64, 4], P('band', 'facet'), may hold values from 0 to 128
- block_weight: float32 [8, 64, 4], P('band', 'facet'), may hold values from 0 to 1
- vis_pos: float32 [8, 64, 4, 2, 2048], P('band', 'facet'), may hold values from 0 to 1
Outputs:
- subgrids: bfloat16 [8, 128, 2, 16, 256], P('band', 'facet')
- visibilities: float32 [8, 64, 4, 2, 2048], P('band', 'facet')
Inputs may be any that keep to these rules, and one draw needn't show every extreme that they name: `slot_of_subgrid`: values are distinct; at most 2 subgrids share an owner, and some owner holds 2.
All inputs are finite; a program needn't handle non-finite values.
Results may differ from a plain program's by a relative error of at most 0.009.
Values may be sent and summed in bfloat16 or wider, within the bound.
A program may use at most 64 MiB of HBM per device.

v0:
```python
import math

import jax
import jax.numpy as jnp
from jax import lax
from jax.sharding import PartitionSpec as P

SG = 256
CR = 16
CAP = 2
PC = 128


kernel_sigma = 1.5


def from_everyone(array, axis):
    size = lax.axis_size(axis)
    return lax.all_to_all(
        jnp.broadcast_to(array[None], (size, *array.shape)), axis, 0, 0, tiled=True
    )


def joined_along(pieces, dim):
    pieces = jnp.moveaxis(pieces, 0, dim)
    lengths = pieces.shape
    return pieces.reshape(*lengths[:dim], lengths[dim] * lengths[dim + 1], *lengths[dim + 2 :])


def collect(array, axis, dim):
    pieces = from_everyone(array, axis)
    return joined_along(pieces, dim)


def column_table(length, width):
    rows = jnp.arange(length, dtype=jnp.int32)[:, None]
    cols = jnp.arange(width, dtype=jnp.int32)[None, :]
    angle = 2.0 * math.pi / length * (rows * cols % length).astype(jnp.float32)
    return jnp.concatenate([jnp.cos(angle), -jnp.sin(angle)], axis=1).astype(jnp.bfloat16)


def combine(product, height, width):
    real_part = product[..., :height, :width] - product[..., height:, width:]
    imag_part = product[..., :height, width:] + product[..., height:, :width]
    return jnp.stack([real_part, imag_part], axis=-3)


def sky_phases(freqs, cells, total):
    angle = 2.0 * math.pi / total * (freqs[..., None] * cells % total).astype(jnp.float32)
    return jnp.concatenate([jnp.cos(angle), -jnp.sin(angle)], axis=-2).astype(jnp.bfloat16)


def inverse_columns(sigma):
    width = sigma.shape[-1]
    index = jnp.arange(width, dtype=jnp.int32)
    angle = 2.0 * math.pi / width * (index[:, None] * index[None, :] % width).astype(jnp.float32)
    cos_part = jnp.cos(angle) / math.sqrt(width)
    sin_part = jnp.sin(angle) / math.sqrt(width)
    real_in = sigma[..., 0, :, :]
    imag_in = sigma[..., 1, :, :]
    real_part = jnp.matmul(real_in, cos_part) - jnp.matmul(imag_in, sin_part)
    imag_part = jnp.matmul(real_in, sin_part) + jnp.matmul(imag_in, cos_part)
    return jnp.stack([real_part, imag_part], axis=-3).astype(jnp.bfloat16)


def degrid_block(patch, position):
    row_grid = jnp.arange(patch.shape[1], dtype=jnp.float32)[:, None]
    col_grid = jnp.arange(patch.shape[2], dtype=jnp.float32)[:, None]
    row_diff = row_grid - position[0][None, :] * (patch.shape[1] - 1)
    col_diff = col_grid - position[1][None, :] * (patch.shape[2] - 1)
    row_kernel = jnp.exp(-row_diff * row_diff / (2.0 * kernel_sigma * kernel_sigma))
    col_kernel = jnp.exp(-col_diff * col_diff / (2.0 * kernel_sigma * kernel_sigma))
    partial_sum = jnp.einsum("xrc,rv->xcv", patch, row_kernel)
    return jnp.sum(partial_sum * col_kernel[None], axis=1)


def local(
    facets, col_window, slot_of_subgrid, block_slot, block_band, block_offset, block_weight, vis_pos
):
    facet_count = lax.axis_size("facet")
    facet_index = lax.axis_index("facet")
    strip_rows = facets.shape[3]
    strip_length = facets.shape[4]
    subgrid_count = slot_of_subgrid.shape[0]
    sky_rows = facet_count * strip_rows
    windowed = (facets[0, 0].astype(jnp.float32) * col_window).astype(jnp.bfloat16)
    windowed = windowed.reshape(2 * strip_rows, strip_length)
    table = column_table(strip_length, SG)
    product = jnp.dot(windowed, table, preferred_element_type=jnp.float32)
    spectrum = (combine(product, strip_rows, SG) * (1.0 / math.sqrt(strip_length))).astype(
        jnp.bfloat16
    )
    spectrum_cat = jnp.concatenate([spectrum[0], spectrum[1]], axis=1)
    cells = facet_index * strip_rows + jnp.arange(strip_rows, dtype=jnp.int32)
    slots = jnp.arange(facet_count * CAP, dtype=jnp.int32)
    match = slot_of_subgrid[None, :] == slots[:, None]
    subgrid_id = jnp.sum(
        jnp.where(match, jnp.arange(subgrid_count, dtype=jnp.int32)[None, :], 0), axis=1
    )
    valid = jnp.any(match, axis=1)
    freqs = subgrid_id[:, None] * CR + jnp.arange(CR, dtype=jnp.int32)[None, :]
    phases = sky_phases(freqs, cells, sky_rows)
    summed = jnp.einsum("akj,jd->akd", phases, spectrum_cat, preferred_element_type=jnp.float32)
    scale = jnp.where(valid, 1.0 / math.sqrt(sky_rows), 0.0).astype(jnp.float32)
    every_slot = (combine(summed, CR, SG) * scale[:, None, None, None]).astype(jnp.bfloat16)
    received = lax.all_to_all(every_slot, "facet", split_axis=0, concat_axis=0, tiled=True)
    sigma = jnp.sum(received.astype(jnp.float32).reshape(facet_count, CAP, 2, CR, SG), axis=0)
    owned = inverse_columns(sigma)
    slot_list = block_slot[0, 0]
    band_list = block_band[0, 0]
    offset_list = block_offset[0, 0]
    zero = jnp.zeros((), jnp.int32)
    every_band = collect(owned[None], "band", 0)

    def fetch(slot, lower_band, start):
        lower = lax.dynamic_slice(
            every_band, (lower_band, slot, zero, zero, start), (1, 1, 2, CR, PC)
        )[0, 0]
        upper = lax.dynamic_slice(
            every_band, (lower_band + 1, slot, zero, zero, start), (1, 1, 2, CR, PC)
        )[0, 0]
        return (lower.astype(jnp.float32), upper.astype(jnp.float32))

    lower_all, upper_all = jax.vmap(fetch)(slot_list, band_list, offset_list)
    weights = block_weight[0, 0][:, None, None, None]
    patches = (1.0 - weights) * lower_all + weights * upper_all
    visible = jax.vmap(degrid_block)(patches, vis_pos[0, 0])
    return (owned[None], visible[None, None])


def solution(mesh):
    in_specs = (
        P("band", "facet", None, None, None),
        P(),
        P(),
        P("band", "facet", None),
        P("band", "facet", None),
        P("band", "facet", None),
        P("band", "facet", None),
        P("band", "facet", None, None, None),
    )
    out_specs = (P("band", "facet", None, None, None), P("band", "facet", None, None, None))
    return jax.shard_map(local, mesh=mesh, in_specs=in_specs, out_specs=out_specs, check_vma=False)
```

profile of v0, /device:TPU:1, one launch (start us, length us, event | category | flops | bytes accessed | tf_op | source)
XLA Modules:
  0.0 127.5 jit_solution(2390654011036893677)
XLA Ops:
  0.6 0.0 copy-start.6
  0.6 0.0 copy-start.4
  0.6 0.0 copy-start.5
  0.7 17.1 %negate_convert_fusion = (bf16[4096,256]{1,0:T(8,128)(2,1)S(1)}, bf16[4096,256]{1,0:T(8,128)(2,1)S(1)}) fusion(), kind=kLoop, calls=%fused_computation.21 | loop fusion | flops 17825792 | bytes 4194304 | tf_op jit(solution)/shard_map/convert.13
  17.8 0.0 copy-done.6
  17.8 0.1 select_reduce_fusion
  17.9 0.1 fusion.62
  18.0 0.0 copy-done.4
  18.0 0.0 copy-done.5
  18.0 1.2 fusion.5
  19.4 4.9 %cosine_convert_fusion.1 = (bf16[128,16,128]{2,0,1:T(8,128)(2,1)S(1)}, bf16[128,16,128]{2,0,1:T(8,128)(2,1)S(1)}) fusion(s32[128]{0:T(128)S(1)} %iota_add_fusion.1, s32[128,16]{0,1:T(8,128)S(1)} %iota_add_fusion), kind=kLoop, calls=%fused_computation.48 | loop fusion | flops 4456448 | bytes 1057280 | tf_op jit(solution)/shard_map/convert.14
  24.3 1.2 fusion.23
  25.6 0.7 fusion.16
  26.3 0.6 fusion.9
  26.9 0.0 copy-start
  26.9 2.5 %copy.29 = bf16[128,2,16,256]{3,2,1,0:T(8,128)(2,1)} copy(bf16[128,2,16,256]{3,0,2,1:T(8,128)(2,1)S(1)} %fusion.9) | data formatting | bytes 4194304 | tf_op jit(solution)/shard_map/convert_element_type | solution.py:105
  29.4 11.6 %all-to-all-start = ((bf16[128,2,16,256]{3,2,1,0:T(8,128)(2,1)}), bf16[128,2,16,256]{3,2,1,0:T(8,128)(2,1)S(1)}, u32[]{:S(2)}, u32[]{:S(2)}) async-start(bf16[128,2,16,256]{3,2,1,0:T(8,128)(2,1)} %copy.29), calls=%async_computation | async-start | bytes 4194304 | tf_op jit(solution)/shard_map/all_to_all | solution.py:106
  41.0 0.0 copy-done
  41.0 0.1 slice_multiply_fusion.1
  41.1 2.8 %fusion.4 = f32[4,128,2048]{2,1,0:T(8,128)} fusion(f32[4,2048]{1,0:T(4,128)S(1)} %get-tuple-element.24), kind=kLoop, calls=%fused_computation.11 | loop fusion | flops 4194304 | bytes 4227072 | tf_op jit(solution)/shard_map/vmap()/exp | solution.py:72
  43.9 0.0 copy-start.7
  43.9 0.0 copy-start.1
  43.9 0.0 copy-start.2
  43.9 0.0 copy-start.3
  43.9 48.3 %all-to-all-done = bf16[128,2,16,256]{3,2,1,0:T(8,128)(2,1)S(1)} async-done(((bf16[128,2,16,256]{3,2,1,0:T(8,128)(2,1)}), bf16[128,2,16,256]{3,2,1,0:T(8,128)(2,1)S(1)}, u32[]{:S(2)}, u32[]{:S(2)}) %all-to-all-start) | async-done | bytes 2097184 | tf_op jit(solution)/shard_map/all_to_all | solution.py:106
  92.2 0.3 convert_reduce_fusion
  92.5 1.1 fusion.41
  93.6 1.1 fusion.37
  94.7 1.1 fusion.18
  95.8 1.1 fusion.19
  97.0 0.7 broadcast_in_dim.28
  97.7 10.0 %all-to-all-start.1 = ((bf16[8,1,2,2,16,256]{5,4,3,2,1,0:T(8,128)(2,1)}), bf16[8,1,2,2,16,256]{5,4,3,2,1,0:T(8,128)(2,1)S(1)}, u32[]{:S(2)}, u32[]{:S(2)}) async-start(bf16[8,1,2,2,16,256]{5,4,3,2,1,0:T(8,128)(2,1)} %broadcast_in_dim.28), calls=%async_computation.1 | async-start | bytes 524288 | tf_op jit(solution)/shard_map/all_to_all | solution.py:19
  107.7 0.0 copy-done.7
  107.8 0.0 copy-done.1
  107.8 0.0 copy-done.2
  107.8 0.0 copy-done.3
  107.8 0.6 copy.37
  108.4 10.3 %all-to-all-done.1 = bf16[8,1,2,2,16,256]{5,4,3,2,1,0:T(8,128)(2,1)S(1)} async-done(((bf16[8,1,2,2,16,256]{5,4,3,2,1,0:T(8,128)(2,1)}), bf16[8,1,2,2,16,256]{5,4,3,2,1,0:T(8,128)(2,1)S(1)}, u32[]{:S(2)}, u32[]{:S(2)}) %all-to-all-start.1) | async-done | bytes 262176 | tf_op jit(solution)/shard_map/all_to_all | solution.py:19
  118.8 1.8 %copy.34 = bf16[8,1,2,2,16,256]{4,3,2,0,5,1:T(2,128)(2,1)S(1)} copy(bf16[8,1,2,2,16,256]{5,4,3,2,1,0:T(8,128)(2,1)S(1)} %all-to-all-done.1) | data formatting | bytes 524288 | tf_op jit(solution)/shard_map/all_to_all | solution.py:19
  120.6 1.2 gather_fusion
  121.8 0.1 copy.35
  121.9 1.3 gather_fusion.1
  123.2 0.1 copy.36
  123.3 4.2 %multiply_reduce_fusion = f32[4,2,2048]{2,1,0:T(2,128)} fusion(f32[4,128,2048]{2,1,0:T(8,128)} %fusion.4, f32[4,2048]{1,0:T(4,128)S(1)} %get-tuple-element.25, bf16[4,2,16,128]{3,2,1,0:T(8,128)(2,1)S(1)} %copy.36, bf16[4,2,16,128]{3,2,1,0:T(8,128)(2,1)S(1)} %copy.35, f32[4]{0:T(128)S(1)} %bitcast.102, f32[4]{0:T(128)S(1)} %broadcast_subtract_fusion), kind=kOutput, calls=%fused_computation.2 | convolution fusion | flops 71892992 | bytes 4358176 | tf_op jit(solution)/shard_map/vmap(xrc,rv->xcv)/dot_general | solution.py:73
  (13 shorter events, 0.1 us)
Async XLA Ops:
  0.6 17.2 %copy-start.6 = (s32[96]{0:T(128)S(1)}, s32[96]{0:T(128)}, u32[]{:S(2)}) copy-start(s32[96]{0:T(128)} %param.10) | copy-start | bytes 1156
  0.6 17.4 %copy-start.4 = (bf16[1,1,2,128,4096]{4,3,2,1,0:T(8,128)(2,1)S(1)}, bf16[1,1,2,128,4096]{4,3,2,1,0:T(8,128)(2,1)}, u32[]{:S(2)}) copy-start(bf16[1,1,2,128,4096]{4,3,2,1,0:T(8,128)(2,1)} %param.8) | copy-start | bytes 6291460
  0.6 17.4 %copy-start.5 = (f32[4096]{0:T(1024)S(1)}, f32[4096]{0:T(1024)}, u32[]{:S(2)}) copy-start(f32[4096]{0:T(1024)} %param.9) | copy-start | bytes 49156
  26.9 14.1 %copy-start = (f32[1,1,4,2,2048]{4,3,2,1,0:T(2,128)S(1)}, f32[1,1,4,2,2048]{4,3,2,1,0:T(2,128)}, u32[]{:S(2)}) copy-start(f32[1,1,4,2,2048]{4,3,2,1,0:T(2,128)} %param.15) | copy-start | bytes 196612
  29.4 62.8 %all-to-all-start = ((bf16[128,2,16,256]{3,2,1,0:T(8,128)(2,1)}), bf16[128,2,16,256]{3,2,1,0:T(8,128)(2,1)S(1)}, u32[]{:S(2)}, u32[]{:S(2)}) async-start(bf16[128,2,16,256]{3,2,1,0:T(8,128)(2,1)} %copy.29), calls=%async_computation | async-start | bytes 4194304 | tf_op jit(solution)/shard_map/all_to_all | solution.py:106
  43.9 63.8 %copy-start.7 = (f32[1,1,4]{2,1,0:T(1,128)S(1)}, f32[1,1,4]{2,1,0:T(1,128)}, u32[]{:S(2)}) copy-start(f32[1,1,4]{2,1,0:T(1,128)} %param.14) | copy-start | bytes 52
  43.9 63.9 %copy-start.1 = (s32[1,1,4]{2,1,0:T(1,128)S(1)}, s32[1,1,4]{2,1,0:T(1,128)}, u32[]{:S(2)}) copy-start(s32[1,1,4]{2,1,0:T(1,128)} %param.12) | copy-start | bytes 52
  43.9 63.9 %copy-start.2 = (s32[1,1,4]{2,1,0:T(1,128)S(1)}, s32[1,1,4]{2,1,0:T(1,128)}, u32[]{:S(2)}) copy-start(s32[1,1,4]{2,1,0:T(1,128)} %param.13) | copy-start | bytes 52
  43.9 63.9 %copy-start.3 = (s32[1,1,4]{2,1,0:T(1,128)S(1)}, s32[1,1,4]{2,1,0:T(1,128)}, u32[]{:S(2)}) copy-start(s32[1,1,4]{2,1,0:T(1,128)} %param.11) | copy-start | bytes 52
  97.7 21.1 %all-to-all-start.1 = ((bf16[8,1,2,2,16,256]{5,4,3,2,1,0:T(8,128)(2,1)}), bf16[8,1,2,2,16,256]{5,4,3,2,1,0:T(8,128)(2,1)S(1)}, u32[]{:S(2)}, u32[]{:S(2)}) async-start(bf16[8,1,2,2,16,256]{5,4,3,2,1,0:T(8,128)(2,1)} %broadcast_in_dim.28), calls=%async_computation.1 | async-start | bytes 524288 | tf_op jit(solution)/shard_map/all_to_all | solution.py:19
where the time goes:
time: 128 us
  waiting for transfers between devices  58.6 us (46%)
  other arithmetic  26.8 us (21%)
  starting transfers between devices  21.7 us (17%)
  matrix products  11.1 us (9%)
  local copies, waits for them, and re-layouts  8.46 us (7%)
    all_to_all x1, waiting for transfers between devices, local(): lax.all_to_all(every_slot, 'facet', split_axis=0, concat_axis=0, tiled=True)  48.3 us
    another operation x2, other arithmetic  22.1 us
    all_to_all x1, starting transfers between devices, local(): lax.all_to_all(every_slot, 'facet', split_axis=0, concat_axis=0, tiled=True)  11.6 us
    all_to_all x1, waiting for transfers between devices, from_everyone(): lax.all_to_all(jnp.broadcast_to(array[None], (size, *array.shape)), axis,...  10.3 us
    all_to_all x1, starting transfers between devices, from_everyone(): lax.all_to_all(jnp.broadcast_to(array[None], (size, *array.shape)), axis,...  10 us
    dot_general x1, matrix products, degrid_block(): partial_sum = jnp.einsum('xrc,rv->xcv', patch, row_kernel)  4.24 us
    exp x1, other arithmetic, degrid_block(): jnp.exp(-col_diff * col_diff / (2.0 * kernel_sigma * kernel_sigma))  2.77 us
  transfers between devices with their start and end apart: 2, of which 2 were waited for; matrix products, arithmetic and copies ran while one was open for 3% of the time, Pallas kernels for 0%

commit v1 on v0

v1 whole, which is shorter than its diff:
```python
import math

import jax
import jax.numpy as jnp
import numpy as np
from jax import lax
from jax.experimental import pallas as pl
from jax.experimental.pallas import tpu as pltpu
from jax.sharding import PartitionSpec as P

BF = jnp.bfloat16
F32 = jnp.float32
MESH = pl.DeviceIdType.MESH

SR = 128
SL = 4096
SG = 256
CR = 16
PC = 128
NS = 96
VB = 4
NV = 2048
NX, NY, NC = 4, 8, 2
NF = NX * NY * NC
NB = 8
COLS = SG // NF
CHUNK = NF // NX
K1 = 64
KH = K1 // CR
K2 = 32
SIGMA = 1.5


def tables():
    n = np.arange(SL)
    c = np.arange(SG)
    d = np.exp(2j * np.pi * ((c[None, :] * n[:, None]) % SL) / SL).sum(1)
    d = d / (math.sqrt(SL) * math.sqrt(SG))
    lanes = np.arange(2 * SL)
    first = np.stack([d[(16 * col - lanes) % SL] for col in range(2 * COLS)])
    first = first.reshape(2, COLS, 2 * SL)
    base = np.stack([first.real, first.imag], axis=1).reshape(4 * COLS, 2 * SL)

    k1 = np.arange(K1)
    f = np.arange(NF)
    w = np.exp(-2j * np.pi * ((k1[:, None] * f[None, :]) % NF) / NF) / math.sqrt(NF)
    w = w.reshape(KH, CR, NF)
    eye = np.eye(COLS)
    parts = [[w.real, -w.imag], [w.imag, w.real]]
    over_facets = np.zeros((2, KH, COLS, CR, NF, 2, COLS))
    for o in range(2):
        for i in range(2):
            over_facets[o, :, :, :, :, i, :] = np.einsum("hrf,cd->hcrfd", parts[o][i], eye)
    over_facets = over_facets.reshape(2 * KH * COLS * CR, NF * 2 * COLS)

    j = np.arange(SR)
    t = np.exp(-2j * np.pi * (k1[:, None] * j[None, :]) / (K1 * SR)).reshape(KH, 1, CR, SR)
    t = np.broadcast_to(t, (KH, COLS, CR, SR)).reshape(KH * COLS * CR, SR)
    twiddle = np.stack([t.real, t.imag])

    k2 = np.arange(K2)
    v = np.exp(-2j * np.pi * ((k2[:, None] * j[None, :]) % SR) / SR) / math.sqrt(SR)
    v = np.where(k2[:, None] < NS // KH, v, 0)
    over_rows = np.concatenate([v.real, v.imag], axis=1)

    order = np.zeros((NS, KH * K2))
    for s in range(NS):
        order[s, (s % KH) * K2 + s // KH] = 1.0
    return base, over_facets, twiddle, over_rows, order


def wait_for(ref, sem):
    pltpu.make_async_copy(ref, ref, sem).wait()


def kernel(
    facets, window, base, over_facets, twiddle, over_rows, order, slots,
    block_slot, block_band, block_offset, block_weight, vis_pos,
    subgrids, visible,
    raw, table, base_v, win_v, over_facets_v, twiddle_v, over_rows_v, order_v, slots_v,
    slot_s, band_s, offset_s, weight_s, pos_v,
    send1, recv1, send2, held, pick, col_kernel, row_kernel,
    raw_sem, const_sem, own_sem, send1_sem, recv1_sem, send2_sem, recv2_sem, send3_sem, recv3_sem,
):
    me = lax.axis_index("facet")
    band = lax.axis_index("band")
    x = me // (NY * NC)
    y = (me // NC) % NY
    core = me % NC

    def facet_at(dx, i):
        k = i // 2
        dy = 4 + (k // 2 + k % 2) * (1 - 2 * (k % 2))
        px = lax.rem(x + dx, NX)
        py = lax.rem(y + dy, NY)
        pc = lax.rem(core + 1 - i % 2, NC)
        return (px * NY + py) * NC + pc

    def each_peer(dx, do):
        def body(i, carry):
            do(facet_at(dx, i))
            return carry

        lax.fori_loop(0, CHUNK if dx else CHUNK - 1, body, 0)

    barrier = pltpu.get_barrier_semaphore()
    for dx in (2, 1, 3, 0):
        each_peer(
            dx,
            lambda p: pl.semaphore_signal(
                barrier, inc=1, device_id=(band, p), device_id_type=MESH
            ),
        )
    for i in range(1, NB):
        pl.semaphore_signal(
            barrier, inc=1, device_id=(lax.rem(band + i, NB), me), device_id_type=MESH
        )

    consts = [
        pltpu.make_async_copy(src, dst, const_sem.at[i])
        for i, (src, dst) in enumerate(
            (
                (base, base_v), (window, win_v), (over_facets, over_facets_v),
                (twiddle, twiddle_v), (over_rows, over_rows_v), (order, order_v),
                (slots, slots_v), (block_slot, slot_s), (block_band, band_s),
                (block_offset, offset_s), (block_weight, weight_s), (vis_pos, pos_v),
            )
        )
    ]
    consts[0].start()
    quarter = SL // 4
    loads = [
        pltpu.make_async_copy(
            facets.at[:, :, pl.ds(quarter * i, quarter)],
            raw.at[:, :, pl.ds(quarter * i, quarter)],
            raw_sem.at[i],
        )
        for i in range(4)
    ]
    consts[1].start()
    for copy in loads:
        copy.start()
    for copy in consts[2:]:
        copy.start()

    consts[0].wait()

    def fill(a, carry):
        start = pl.multiple_of(SL - 128 * a, 128)
        row = pl.multiple_of(16 * a, 16)
        table[pl.ds(row, 16), :] = base_v[:, pl.ds(start, SL)]
        return carry

    lax.fori_loop(0, 4 * NF * COLS * 2 // 64, fill, 0)

    consts[1].wait()
    total = None
    for i in range(4):
        loads[i].wait()
        cut = pl.ds(quarter * i, quarter)
        windowed = (raw[:, :, cut].astype(F32) * win_v[:, cut][None]).astype(BF)
        windowed = windowed.reshape(2 * SR, quarter)
        product = lax.dot_general(
            table[:, cut], windowed, (((1,), (1,)), ((), ())), preferred_element_type=F32
        )
        total = product if total is None else total + product
    from_real = total[:, :SR].reshape(NF, 2 * COLS, SR)
    from_imag = total[:, SR:].reshape(NF, 2 * COLS, SR)
    swapped = pltpu.roll(from_imag, COLS, 1)
    part = lax.broadcasted_iota(jnp.int32, swapped.shape, 1)
    send1[...] = (from_real + jnp.where(part < COLS, -swapped, swapped)).astype(BF)

    pl.semaphore_wait(barrier, NF - 1 + NB - 1)

    for dx in (2, 1, 3, 0):
        each_peer(
            dx,
            lambda p: pltpu.make_async_remote_copy(
                send1.at[p], recv1.at[me], send1_sem, recv1_sem,
                device_id=(band, p), device_id_type=MESH,
            ).start(),
        )
    own1 = pltpu.make_async_copy(send1.at[me], recv1.at[me], own_sem.at[0])
    own1.start()

    for copy in consts[2:]:
        copy.wait()
    named = lax.broadcasted_iota(jnp.int32, (2 * NF, NS), 0) == slots_v[...]
    choose = jnp.dot(
        jnp.where(named, 1.0, 0.0).astype(BF), order_v[...], preferred_element_type=F32
    ).astype(BF)
    scale = 1.0 / (2.0 * SIGMA * SIGMA)
    rows = lax.broadcasted_iota(jnp.int32, (CR, NV), 0).astype(F32)
    cols = lax.broadcasted_iota(jnp.int32, (PC, 512), 0).astype(F32)
    for v in range(VB):
        dr = rows - pos_v[v, 0:1, :] * (CR - 1)
        row_kernel[v] = jnp.exp(-dr * dr * scale)

        def gauss(i, carry, v=v):
            cut = pl.ds(pl.multiple_of(512 * i, 512), 512)
            dc = cols - pos_v[v, 1:2, cut] * (PC - 1)
            col_kernel[v // 2, pl.ds(PC * (v % 2), PC), cut] = jnp.exp(-dc * dc * scale).astype(BF)
            return carry

        lax.fori_loop(0, NV // 512, gauss, 0)
        source = lax.broadcasted_iota(jnp.int32, (2 * NF, PC), 0)
        q = lax.broadcasted_iota(jnp.int32, (2 * NF, PC), 1)
        for c in range(COLS):
            hit = ((source // 2) * COLS + c == q + offset_s[0, 0, v]) & (
                source % 2 == slot_s[0, 0, v]
            )
            pick[v, :, pl.ds(PC * c, PC)] = jnp.where(hit, 1.0, 0.0).astype(BF)

    own1.wait()
    wait_for(recv1.at[pl.ds(0, NF - 1)], recv1_sem)
    arrived = recv1[...].astype(F32).reshape(NF * 2 * COLS, SR).astype(BF)
    half = KH * COLS * CR
    over = jnp.dot(over_facets_v[...], arrived, preferred_element_type=F32)
    yr, yi = over[:half], over[half:]
    tr, ti = twiddle_v[0], twiddle_v[1]
    zr = (yr * tr - yi * ti).astype(BF)
    zi = (yi * tr + yr * ti).astype(BF)
    block = COLS * CR
    turned = jnp.concatenate(
        [
            piece
            for h in range(KH)
            for piece in (
                jnp.concatenate([zr[h * block : (h + 1) * block], -zi[h * block : (h + 1) * block]], 1),
                jnp.concatenate([zi[h * block : (h + 1) * block], zr[h * block : (h + 1) * block]], 1),
            )
        ],
        axis=0,
    )
    grid = lax.dot_general(
        over_rows_v[...], turned, (((1,), (1,)), ((), ())), preferred_element_type=F32
    )
    by_subgrid = jnp.concatenate(
        [grid[:, 2 * block * h : 2 * block * (h + 1)] for h in range(KH)], axis=0
    ).astype(BF)
    by_slot = jnp.dot(choose, by_subgrid, preferred_element_type=F32)
    send2[...] = by_slot.reshape(NF, 2, 2 * block).astype(BF)

    for dx in (2, 1, 3, 0):
        each_peer(
            dx,
            lambda p, dx=dx: pltpu.make_async_remote_copy(
                send2.at[p], held.at[band, me], send2_sem, recv2_sem.at[dx],
                device_id=(band, p), device_id_type=MESH,
            ).start(),
        )
    own2 = pltpu.make_async_copy(send2.at[me], held.at[band, me], own_sem.at[1])
    own2.start()
    own2.wait()
    for dx in (0, 1, 3, 2):
        count = CHUNK if dx else CHUNK - 1
        wait_for(send2.at[pl.ds(0, count)], recv2_sem.at[dx])
        piece = pl.ds(pl.multiple_of(lax.rem(x + NX - dx, NX) * CHUNK, CHUNK), CHUNK)
        for i in (4, 3, 5, 2, 6, 1, 7):
            pltpu.make_async_remote_copy(
                held.at[band, piece], held.at[band, piece], send3_sem, recv3_sem,
                device_id=(lax.rem(band + i, NB), me), device_id_type=MESH,
            ).start()

    def spread(values, selector):
        return lax.dot_general(
            values, selector, (((0,), (0,)), ((), ())), preferred_element_type=F32
        )

    def joined(rows_by, width):
        return [
            sum(
                rows_by[p * block + c * CR : p * block + (c + 1) * CR, width * c : width * (c + 1)]
                for c in range(COLS)
            )
            for p in range(2)
        ]

    own = held[band].astype(F32).reshape(2 * NF, 2 * block).astype(BF)
    source = lax.broadcasted_iota(jnp.int32, (2 * NF, SG), 0)
    column = lax.broadcasted_iota(jnp.int32, (2 * NF, SG), 1)
    for slot in range(2):
        selector = jnp.concatenate(
            [
                jnp.where(
                    ((source // 2) * COLS + c == column) & (source % 2 == slot), 1.0, 0.0
                ).astype(BF)
                for c in range(COLS)
            ],
            axis=1,
        )
        pieces = joined(spread(own, selector), SG)
        for p in range(2):
            subgrids[slot, p] = pieces[p].astype(BF)

    wait_for(held.at[pl.ds(0, NB - 1)], recv3_sem)
    nothing = jnp.zeros((2 * CR, PC), BF)
    for pair in range(VB // 2):
        patches = []
        for v in (2 * pair, 2 * pair + 1):
            lo = band_s[0, 0, v]
            weight = weight_s[0, 0, v]
            mixed = (1.0 - weight) * held[lo].astype(F32) + weight * held[lo + 1].astype(F32)
            mixed = mixed.reshape(2 * NF, 2 * block).astype(BF)
            pieces = joined(spread(mixed, pick[v]), PC)
            patches.append(jnp.concatenate(pieces, axis=0).astype(BF))
        left = jnp.concatenate(
            [
                jnp.concatenate([patches[0], nothing], 1),
                jnp.concatenate([nothing, patches[1]], 1),
            ],
            axis=0,
        )
        summed = jnp.dot(left, col_kernel[pair], preferred_element_type=F32)
        for b in range(2):
            v = 2 * pair + b
            for p in range(2):
                at = (2 * b + p) * CR
                visible[v, p : p + 1, :] = jnp.sum(
                    summed[at : at + CR] * row_kernel[v], axis=0, keepdims=True
                )

    wait_for(send1.at[pl.ds(0, NF - 1)], send1_sem)
    wait_for(send2.at[pl.ds(0, NF - 1)], send2_sem)
    wait_for(held.at[pl.ds(0, NB - 1)], send3_sem)


def local(
    facets, col_window, slot_of_subgrid, block_slot, block_band, block_offset, block_weight, vis_pos
):
    base, over_facets, twiddle, over_rows, order = tables()
    anywhere = pl.BlockSpec(memory_space=pl.ANY)
    whole = pl.BlockSpec(memory_space=pltpu.VMEM)
    dma = pltpu.SemaphoreType.DMA
    vmem = pltpu.VMEM
    half = KH * COLS * CR
    args = (
        facets[0, 0],
        col_window[None],
        jnp.asarray(base, BF),
        jnp.asarray(over_facets, BF),
        jnp.asarray(twiddle, F32),
        jnp.asarray(over_rows, BF),
        jnp.asarray(order, BF),
        slot_of_subgrid[None],
        block_slot,
        block_band,
        block_offset,
        block_weight,
        vis_pos[0, 0],
    )
    subgrids, visible = pl.pallas_call(
        kernel,
        out_shape=(
            jax.ShapeDtypeStruct((2, 2, CR, SG), BF),
            jax.ShapeDtypeStruct((VB, 2, NV), F32),
        ),
        in_specs=[anywhere] * len(args),
        out_specs=(whole, whole),
        scratch_shapes=[
            vmem((2, SR, SL), BF),
            vmem((NF * 2 * COLS, SL), BF),
            vmem((4 * COLS, 2 * SL), BF),
            vmem((1, SL), F32),
            vmem((2 * half, NF * 2 * COLS), BF),
            vmem((2, half, SR), F32),
            vmem((K2, 2 * SR), BF),
            vmem((NS, KH * K2), BF),
            vmem((1, NS), jnp.int32),
            pltpu.SMEM((1, 1, VB), jnp.int32),
            pltpu.SMEM((1, 1, VB), jnp.int32),
            pltpu.SMEM((1, 1, VB), jnp.int32),
            pltpu.SMEM((1, 1, VB), F32),
            vmem((VB, 2, NV), F32),
            vmem((NF, 2 * COLS, SR), BF),
            vmem((NF, 2 * COLS, SR), BF),
            vmem((NF, 2, 2 * COLS * CR), BF),
            vmem((NB, NF, 2, 2 * COLS * CR), BF),
            vmem((VB, 2 * NF, COLS * PC), BF),
            vmem((VB // 2, 2 * PC, NV), BF),
            vmem((VB, CR, NV), F32),
            dma((4,)),
            dma((12,)),
            dma((2,)),
            dma,
            dma,
            dma,
            dma((NX,)),
            dma,
            dma,
        ],
        compiler_params=pltpu.CompilerParams(collective_id=0, has_side_effects=True),
        name="column_pass",
    )(*args)
    return subgrids[None], visible[None, None]


def solution(mesh):
    in_specs = (
        P("band", "facet", None, None, None),
        P(),
        P(),
        P("band", "facet", None),
        P("band", "facet", None),
        P("band", "facet", None),
        P("band", "facet", None),
        P("band", "facet", None, None, None),
    )
    out_specs = (P("band", "facet", None, None, None), P("band", "facet", None, None, None))
    return jax.shard_map(local, mesh=mesh, in_specs=in_specs, out_specs=out_specs, check_vma=False)
```

time: 128 us -> 44 us (0.34)
  waiting for transfers between devices: 58.6 us -> 0 us
  Pallas kernels: 0 us -> 40.3 us
  other arithmetic: 26.8 us -> 0 us
  starting transfers between devices: 21.7 us -> 0 us
  matrix products: 11.1 us -> 0 us
  local copies, waits for them, and re-layouts: 8.46 us -> 2.85 us
    all_to_all x2 -> x0, waiting for transfers between devices: 58.6 us -> none  [the longest x1 48.3 us: local(): lax.all_to_all(every_slot, 'facet', split_axis=0, concat_axis=0, tiled=True)]
    pallas_call x0 -> x1, Pallas kernels: none -> 40.3 us  [local(): pl.pallas_call(kernel, out_shape=(jax.ShapeDtypeStruct((2, 2, CR, SG), BF...]
    another operation x6 -> x0, other arithmetic: 22.8 us -> none
    all_to_all x2 -> x0, starting transfers between devices: 21.7 us -> none  [the longest x1 11.6 us: local(): lax.all_to_all(every_slot, 'facet', split_axis=0, concat_axis=0, tiled=True)]
    dot_general x7 -> x0, matrix products: 11.1 us -> none  [the longest x1 4.24 us: degrid_block(): partial_sum = jnp.einsum('xrc,rv->xcv', patch, row_kernel)]
    exp x1 -> x0, other arithmetic: 2.77 us -> none  [degrid_block(): jnp.exp(-col_diff * col_diff / (2.0 * kernel_sigma * kernel_sigma))]
    gather x4 -> x0, local copies, waits for them, and re-layouts: 2.72 us -> none  [the longest x2 1.37 us: fetch(): lax.dynamic_slice(every_band, (lower_band + 1, slot, zero, zero, start),...]
    convert_element_type x1 -> x0, local copies, waits for them, and re-layouts: 2.5 us -> none  [local(): (combine(summed, CR, SG) * scale[:, None, None, None]).astype(jnp.bfloat16)]
  transfers between devices with their start and end apart: 2 -> 0, of which waited for: 2 -> 0; matrix products, arithmetic and copies ran while one was open for 3% -> 0% of each run, Pallas kernels for 0% -> 0%
where the time goes in v1:
time: 44 us; the launch traced here: 43.8 us
  Pallas kernels  40.3 us (92%)
  local copies, waits for them, and re-layouts  2.85 us (6%)
  between operations  0.64 us (1%)
    pallas_call x1, Pallas kernels, local(): pl.pallas_call(kernel, out_shape=(jax.ShapeDtypeStruct((2, 2, CR, SG), BF...  40.3 us
    unnamed x2, local copies, waits for them, and re-layouts  2.85 us

profile of v1, /device:TPU:1, one launch (start us, length us, event | category | flops | bytes accessed | tf_op | source)
XLA Modules:
  0.0 43.8 jit_solution(687465554659793150)
XLA Ops:
  0.6 40.3 %column_pass.1 = (bf16[2,2,16,256]{3,2,1,0:T(8,128)(2,1)}, f32[4,2,2048]{2,1,0:T(2,128)}) custom-call(bf16[2,128,4096]{2,1,0:T(8,128)(2,1)} %bitcast.6, f32[1,4096]{1,0:T(1,128)} %bitcast.10, bf16[16,8192]{1,0:T(8,128)(2,1)} %constant.10.clone.base, bf16[512,512]{1,0:T(8,128)(2,1)} %constant.11.clone.over_facets, f32[2,256,128]{2,1,0:T(8,128)} %constant.12.clone.twiddle, ...), custom_call_target="tpu_custom_call" | custom-call | tf_op jit(solution)/shard_map/column_pass/pallas_call | solution.py:352
  41.0 1.4 %copy.17 = bf16[1,2,2,16,256]{4,3,2,1,0:T(8,128)(2,1)} copy(bf16[1,2,2,16,256]{4,3,2,1,0:T(8,128)(2,1)} %bitcast.9) | data formatting | bytes 65536
  42.3 1.5 %copy.18 = f32[1,1,4,2,2048]{4,3,2,1,0:T(2,128)} copy(f32[1,1,4,2,2048]{4,3,2,1,0:T(2,128)} %bitcast.8) | data formatting | bytes 131072

commit v2 on v1

--- a/solution.py
+++ b/solution.py
@@ -29,6 +29,18 @@
 KH = K1 // CR
 K2 = 32
 SIGMA = 1.5
+BLOCK = COLS * CR
+HALF = KH * BLOCK
+PEERS = sorted(
+    (
+        (dx, dy, dc)
+        for dx in range(NX)
+        for dy in range(NY)
+        for dc in range(NC)
+        if dx or dy or dc
+    ),
+    key=lambda t: -(4 * min(t[0], NX - t[0]) + 4 * min(t[1], NY - t[1]) + t[2]),
+)
 
 
 def tables():
@@ -73,13 +85,29 @@
     pltpu.make_async_copy(ref, ref, sem).wait()
 
 
-def kernel(
+def spread(values, selector):
+    return lax.dot_general(
+        values, selector, (((0,), (0,)), ((), ())), preferred_element_type=F32
+    )
+
+
+def joined(rows_by, width):
+    return [
+        sum(
+            rows_by[p * BLOCK + c * CR : p * BLOCK + (c + 1) * CR, width * c : width * (c + 1)]
+            for c in range(COLS)
+        )
+        for p in range(2)
+    ]
+
+
+def exchange_kernel(
     facets, window, base, over_facets, twiddle, over_rows, order, slots,
-    block_slot, block_band, block_offset, block_weight, vis_pos,
-    subgrids, visible,
+    block_slot, block_offset, vis_pos,
+    held, pick, col_kernel, row_kernel, subgrids,
     raw, table, base_v, win_v, over_facets_v, twiddle_v, over_rows_v, order_v, slots_v,
-    slot_s, band_s, offset_s, weight_s, pos_v,
-    send1, recv1, send2, held, pick, col_kernel, row_kernel,
+    slot_s, offset_s, pos_v,
+    send1, recv1, send2,
     raw_sem, const_sem, own_sem, send1_sem, recv1_sem, send2_sem, recv2_sem, send3_sem, recv3_sem,
 ):
     me = lax.axis_index("facet")
@@ -88,33 +116,13 @@
     y = (me // NC) % NY
     core = me % NC
 
-    def facet_at(dx, i):
-        k = i // 2
-        dy = 4 + (k // 2 + k % 2) * (1 - 2 * (k % 2))
-        px = lax.rem(x + dx, NX)
-        py = lax.rem(y + dy, NY)
-        pc = lax.rem(core + 1 - i % 2, NC)
-        return (px * NY + py) * NC + pc
-
-    def each_peer(dx, do):
-        def body(i, carry):
-            do(facet_at(dx, i))
-            return carry
-
-        lax.fori_loop(0, CHUNK if dx else CHUNK - 1, body, 0)
-
-    barrier = pltpu.get_barrier_semaphore()
-    for dx in (2, 1, 3, 0):
-        each_peer(
-            dx,
-            lambda p: pl.semaphore_signal(
-                barrier, inc=1, device_id=(band, p), device_id_type=MESH
-            ),
-        )
-    for i in range(1, NB):
-        pl.semaphore_signal(
-            barrier, inc=1, device_id=(lax.rem(band + i, NB), me), device_id_type=MESH
-        )
+    rows_of = [lax.rem(x + dx, NX) * (NY * NC) for dx in range(NX)]
+    places = [lax.rem(y + dy, NY) * NC for dy in range(NY)]
+    cores = [core, 1 - core]
+
+    def each_peer(do):
+        for dx, dy, dc in PEERS:
+            do(dx, rows_of[dx] + places[dy] + cores[dc])
 
     consts = [
         pltpu.make_async_copy(src, dst, const_sem.at[i])
@@ -122,8 +130,8 @@
             (
                 (base, base_v), (window, win_v), (over_facets, over_facets_v),
                 (twiddle, twiddle_v), (over_rows, over_rows_v), (order, order_v),
-                (slots, slots_v), (block_slot, slot_s), (block_band, band_s),
-                (block_offset, offset_s), (block_weight, weight_s), (vis_pos, pos_v),
+                (slots, slots_v), (block_slot, slot_s), (block_offset, offset_s),
+                (vis_pos, pos_v),
             )
         )
     ]
@@ -140,18 +148,23 @@
     consts[1].start()
     for copy in loads:
         copy.start()
+
+    barrier = pltpu.get_barrier_semaphore()
+    each_peer(
+        lambda dx, p: pl.semaphore_signal(
+            barrier, inc=1, device_id=(band, p), device_id_type=MESH
+        )
+    )
+    for i in range(1, NB):
+        pl.semaphore_signal(
+            barrier, inc=1, device_id=(lax.rem(band + i, NB), me), device_id_type=MESH
+        )
     for copy in consts[2:]:
         copy.start()
 
     consts[0].wait()
-
-    def fill(a, carry):
-        start = pl.multiple_of(SL - 128 * a, 128)
-        row = pl.multiple_of(16 * a, 16)
-        table[pl.ds(row, 16), :] = base_v[:, pl.ds(start, SL)]
-        return carry
-
-    lax.fori_loop(0, 4 * NF * COLS * 2 // 64, fill, 0)
+    for a in range(SG // (2 * COLS)):
+        table[16 * a : 16 * (a + 1), :] = base_v[:, SL - 128 * a : 2 * SL - 128 * a]
 
     consts[1].wait()
     total = None
@@ -172,14 +185,12 @@
 
     pl.semaphore_wait(barrier, NF - 1 + NB - 1)
 
-    for dx in (2, 1, 3, 0):
-        each_peer(
-            dx,
-            lambda p: pltpu.make_async_remote_copy(
-                send1.at[p], recv1.at[me], send1_sem, recv1_sem,
-                device_id=(band, p), device_id_type=MESH,
-            ).start(),
-        )
+    each_peer(
+        lambda dx, p: pltpu.make_async_remote_copy(
+            send1.at[p], recv1.at[me], send1_sem, recv1_sem,
+            device_id=(band, p), device_id_type=MESH,
+        ).start()
+    )
     own1 = pltpu.make_async_copy(send1.at[me], recv1.at[me], own_sem.at[0])
     own1.start()
 
@@ -214,20 +225,18 @@
     own1.wait()
     wait_for(recv1.at[pl.ds(0, NF - 1)], recv1_sem)
     arrived = recv1[...].astype(F32).reshape(NF * 2 * COLS, SR).astype(BF)
-    half = KH * COLS * CR
     over = jnp.dot(over_facets_v[...], arrived, preferred_element_type=F32)
-    yr, yi = over[:half], over[half:]
+    yr, yi = over[:HALF], over[HALF:]
     tr, ti = twiddle_v[0], twiddle_v[1]
     zr = (yr * tr - yi * ti).astype(BF)
     zi = (yi * tr + yr * ti).astype(BF)
-    block = COLS * CR
     turned = jnp.concatenate(
         [
             piece
             for h in range(KH)
             for piece in (
-                jnp.concatenate([zr[h * block : (h + 1) * block], -zi[h * block : (h + 1) * block]], 1),
-                jnp.concatenate([zi[h * block : (h + 1) * block], zr[h * block : (h + 1) * block]], 1),
+                jnp.concatenate([zr[h * BLOCK : (h + 1) * BLOCK], -zi[h * BLOCK : (h + 1) * BLOCK]], 1),
+                jnp.concatenate([zi[h * BLOCK : (h + 1) * BLOCK], zr[h * BLOCK : (h + 1) * BLOCK]], 1),
             )
         ],
         axis=0,
@@ -236,19 +245,17 @@
         over_rows_v[...], turned, (((1,), (1,)), ((), ())), preferred_element_type=F32
     )
     by_subgrid = jnp.concatenate(
-        [grid[:, 2 * block * h : 2 * block * (h + 1)] for h in range(KH)], axis=0
+        [grid[:, 2 * BLOCK * h : 2 * BLOCK * (h + 1)] for h in range(KH)], axis=0
     ).astype(BF)
     by_slot = jnp.dot(choose, by_subgrid, preferred_element_type=F32)
-    send2[...] = by_slot.reshape(NF, 2, 2 * block).astype(BF)
-
-    for dx in (2, 1, 3, 0):
-        each_peer(
-            dx,
-            lambda p, dx=dx: pltpu.make_async_remote_copy(
-                send2.at[p], held.at[band, me], send2_sem, recv2_sem.at[dx],
-                device_id=(band, p), device_id_type=MESH,
-            ).start(),
-        )
+    send2[...] = by_slot.reshape(NF, 2, 2 * BLOCK).astype(BF)
+
+    each_peer(
+        lambda dx, p: pltpu.make_async_remote_copy(
+            send2.at[p], held.at[band, me], send2_sem, recv2_sem.at[dx],
+            device_id=(band, p), device_id_type=MESH,
+        ).start()
+    )
     own2 = pltpu.make_async_copy(send2.at[me], held.at[band, me], own_sem.at[1])
     own2.start()
     own2.wait()
@@ -256,27 +263,16 @@
         count = CHUNK if dx else CHUNK - 1
         wait_for(send2.at[pl.ds(0, count)], recv2_sem.at[dx])
         piece = pl.ds(pl.multiple_of(lax.rem(x + NX - dx, NX) * CHUNK, CHUNK), CHUNK)
-        for i in (4, 3, 5, 2, 6, 1, 7):
-            pltpu.make_async_remote_copy(
-                held.at[band, piece], held.at[band, piece], send3_sem, recv3_sem,
-                device_id=(lax.rem(band + i, NB), me), device_id_type=MESH,
-            ).start()
-
-    def spread(values, selector):
-        return lax.dot_general(
-            values, selector, (((0,), (0,)), ((), ())), preferred_element_type=F32
-        )
-
-    def joined(rows_by, width):
-        return [
-            sum(
-                rows_by[p * block + c * CR : p * block + (c + 1) * CR, width * c : width * (c + 1)]
-                for c in range(COLS)
-            )
-            for p in range(2)
-        ]
-
-    own = held[band].astype(F32).reshape(2 * NF, 2 * block).astype(BF)
+        for to in range(NB):
+
+            @pl.when(band != to)
+            def _(to=to, piece=piece):
+                pltpu.make_async_remote_copy(
+                    held.at[band, piece], held.at[band, piece], send3_sem, recv3_sem,
+                    device_id=(to, me), device_id_type=MESH,
+                ).start()
+
+    own = held[band].astype(F32).reshape(2 * NF, 2 * BLOCK).astype(BF)
     source = lax.broadcasted_iota(jnp.int32, (2 * NF, SG), 0)
     column = lax.broadcasted_iota(jnp.int32, (2 * NF, SG), 1)
     for slot in range(2):
@@ -294,14 +290,21 @@
             subgrids[slot, p] = pieces[p].astype(BF)
 
     wait_for(held.at[pl.ds(0, NB - 1)], recv3_sem)
+    wait_for(send1.at[pl.ds(0, NF - 1)], send1_sem)
+    wait_for(send2.at[pl.ds(0, NF - 1)], send2_sem)
+    wait_for(held.at[pl.ds(0, NB - 1)], send3_sem)
+
+
+def degrid_kernel(block_band, block_weight, held, pick, col_kernel, row_kernel, own, subgrids, visible):
+    subgrids[...] = own[...]
     nothing = jnp.zeros((2 * CR, PC), BF)
     for pair in range(VB // 2):
         patches = []
         for v in (2 * pair, 2 * pair + 1):
-            lo = band_s[0, 0, v]
-            weight = weight_s[0, 0, v]
+            lo = block_band[0, 0, v]
+            weight = block_weight[0, 0, v]
             mixed = (1.0 - weight) * held[lo].astype(F32) + weight * held[lo + 1].astype(F32)
-            mixed = mixed.reshape(2 * NF, 2 * block).astype(BF)
+            mixed = mixed.reshape(2 * NF, 2 * BLOCK).astype(BF)
             pieces = joined(spread(mixed, pick[v]), PC)
             patches.append(jnp.concatenate(pieces, axis=0).astype(BF))
         left = jnp.concatenate(
@@ -320,20 +323,15 @@
                     summed[at : at + CR] * row_kernel[v], axis=0, keepdims=True
                 )
 
-    wait_for(send1.at[pl.ds(0, NF - 1)], send1_sem)
-    wait_for(send2.at[pl.ds(0, NF - 1)], send2_sem)
-    wait_for(held.at[pl.ds(0, NB - 1)], send3_sem)
-
 
 def local(
     facets, col_window, slot_of_subgrid, block_slot, block_band, block_offset, block_weight, vis_pos
 ):
     base, over_facets, twiddle, over_rows, order = tables()
-    anywhere = pl.BlockSpec(memory_space=pl.ANY)
+    anywhere = pl.BlockSpec(memory_space=pltpu.HBM)
     whole = pl.BlockSpec(memory_space=pltpu.VMEM)
     dma = pltpu.SemaphoreType.DMA
     vmem = pltpu.VMEM
-    half = KH * COLS * CR
     args = (
         facets[0, 0],
         col_window[None],
@@ -344,43 +342,38 @@
         jnp.asarray(order, BF),
         slot_of_subgrid[None],
         block_slot,
-        block_band,
         block_offset,
-        block_weight,
         vis_pos[0, 0],
     )
-    subgrids, visible = pl.pallas_call(
-        kernel,
+    made = pl.pallas_call(
+        exchange_kernel,
         out_shape=(
-            jax.ShapeDtypeStruct((2, 2, CR, SG), BF),
-            jax.ShapeDtypeStruct((VB, 2, NV), F32),
+            vmem((NB, NF, 2, 2 * BLOCK), BF),
+            vmem((VB, 2 * NF, COLS * PC), BF),
+            vmem((VB // 2, 2 * PC, NV), BF),
+            vmem((VB, CR, NV), F32),
+            vmem((2, 2, CR, SG), BF),
         ),
         in_specs=[anywhere] * len(args),
-        out_specs=(whole, whole),
+        out_specs=(whole,) * 5,
         scratch_shapes=[
             vmem((2, SR, SL), BF),
             vmem((NF * 2 * COLS, SL), BF),
             vmem((4 * COLS, 2 * SL), BF),
             vmem((1, SL), F32),
-            vmem((2 * half, NF * 2 * COLS), BF),
-            vmem((2, half, SR), F32),
+            vmem((2 * HALF, NF * 2 * COLS), BF),
+            vmem((2, HALF, SR), F32),
             vmem((K2, 2 * SR), BF),
             vmem((NS, KH * K2), BF),
             vmem((1, NS), jnp.int32),
             pltpu.SMEM((1, 1, VB), jnp.int32),
             pltpu.SMEM((1, 1, VB), jnp.int32),
-            pltpu.SMEM((1, 1, VB), jnp.int32),
-            pltpu.SMEM((1, 1, VB), F32),
             vmem((VB, 2, NV), F32),
             vmem((NF, 2 * COLS, SR), BF),
             vmem((NF, 2 * COLS, SR), BF),
-            vmem((NF, 2, 2 * COLS * CR), BF),
-            vmem((NB, NF, 2, 2 * COLS * CR), BF),
-            vmem((VB, 2 * NF, COLS * PC), BF),
-            vmem((VB // 2, 2 * PC, NV), BF),
-            vmem((VB, CR, NV), F32),
+            vmem((NF, 2, 2 * BLOCK), BF),
             dma((4,)),
-            dma((12,)),
+            dma((10,)),
             dma((2,)),
             dma,
             dma,
@@ -389,9 +382,23 @@
             dma,
             dma,
         ],
-        compiler_params=pltpu.CompilerParams(collective_id=0, has_side_effects=True),
+        compiler_params=pltpu.CompilerParams(
+            collective_id=0, has_side_effects=True, vmem_limit_bytes=24 * 2**20
+        ),
         name="column_pass",
-    )(*args)
+    )(*(pltpu.with_memory_space_constraint(a, pltpu.HBM) for a in args))
+    scalars = pl.BlockSpec(memory_space=pltpu.SMEM)
+    subgrids, visible = pl.pallas_call(
+        degrid_kernel,
+        out_shape=(
+            jax.ShapeDtypeStruct((2, 2, CR, SG), BF),
+            jax.ShapeDtypeStruct((VB, 2, NV), F32),
+        ),
+        in_specs=[scalars, scalars] + [whole] * 5,
+        out_specs=(whole, whole),
+        compiler_params=pltpu.CompilerParams(vmem_limit_bytes=24 * 2**20),
+        name="degrid",
+    )(block_band, block_weight, *made)
     return subgrids[None], visible[None, None]
 
 

time: 44 us -> 39 us (0.89)
  local copies, waits for them, and re-layouts: 2.85 us -> 0.01 us
  Pallas kernels: 40.3 us -> 38.2 us
    unnamed x2 -> x4, local copies, waits for them, and re-layouts: 2.85 us -> 0.01 us
    pallas_call x1 -> x2, Pallas kernels: 40.3 us -> 38.2 us  [the longest x1 36.1 us: local(): pl.pallas_call(exchange_kernel, out_shape=(vmem((NB, NF, 2, 2 * BLOCK), B...]
where the time goes in v2:
time: 39 us; the launch traced here: 38.9 us
  Pallas kernels  38.2 us (98%)
  between operations  0.67 us (2%)
    pallas_call x1, Pallas kernels, local(): pl.pallas_call(exchange_kernel, out_shape=(vmem((NB, NF, 2, 2 * BLOCK), B...  36.1 us
    pallas_call x1, Pallas kernels, local(): pl.pallas_call(degrid_kernel, out_shape=(jax.ShapeDtypeStruct((2, 2, CR,...  2.08 us

profile of v2, /device:TPU:1, one launch (start us, length us, event | category | flops | bytes accessed | tf_op | source)
XLA Modules:
  0.0 38.9 jit_solution(13772137273833251825)
XLA Ops:
  0.6 0.0 copy-start.1
  0.6 0.0 copy-start
  0.7 36.1 %column_pass.1 = (bf16[8,64,2,128]{3,2,1,0:T(2,128)(2,1)S(1)}, bf16[4,128,512]{2,1,0:T(8,128)(2,1)S(1)}, bf16[2,256,2048]{2,1,0:T(8,128)(2,1)S(1)}, f32[4,16,204...) custom-call(bf16[2,128,4096]{2,1,0:T(8,128)(2,1)} %bitcast.6, f32[1,4096]{1,0:T(1,128)} %bitcast.8, ...), custom_call_target="tpu_custom_call" | custom-call | tf_op jit(solution)/shard_map/column_pass/pallas_call | solution.py:348
  36.8 0.0 copy-done.1
  36.8 0.0 copy-done
  36.8 2.1 %degrid.1 = (bf16[2,2,16,256]{3,2,1,0:T(8,128)(2,1)}, f32[4,2,2048]{2,1,0:T(2,128)}) custom-call(s32[1,1,4]{2,1,0:T(1,128)S(1)} %copy-done, f32[1,1,4]{2,1,0:T(1,128)S(1)} %copy-done.1, bf16[8,64,2,128]{3,2,1,0:T(2,128)(2,1)S(1)} %get-tuple-element.9.held, bf16[4,128,512]{2,1,0:T(8,128)(2,1)S(1)} %get-tuple-element.10.pick, ...), custom_call_target="tpu_custom_call" | custom-call | tf_op jit(solution)/shard_map/degrid/pallas_call | solution.py:391
Async XLA Ops:
  0.6 36.2 %copy-start.1 = (f32[1,1,4]{2,1,0:T(1,128)S(1)}, f32[1,1,4]{2,1,0:T(1,128)}, u32[]{:S(2)}) copy-start(f32[1,1,4]{2,1,0:T(1,128)} %block_weight.1) | copy-start | bytes 52
  0.6 36.2 %copy-start = (s32[1,1,4]{2,1,0:T(1,128)S(1)}, s32[1,1,4]{2,1,0:T(1,128)}, u32[]{:S(2)}) copy-start(s32[1,1,4]{2,1,0:T(1,128)} %block_band.1) | copy-start | bytes 52

commit v3 on v2

--- a/solution.py
+++ b/solution.py
@@ -44,14 +44,17 @@
 
 
 def tables():
-    n = np.arange(SL)
-    c = np.arange(SG)
-    d = np.exp(2j * np.pi * ((c[None, :] * n[:, None]) % SL) / SL).sum(1)
-    d = d / (math.sqrt(SL) * math.sqrt(SG))
-    lanes = np.arange(2 * SL)
-    first = np.stack([d[(16 * col - lanes) % SL] for col in range(2 * COLS)])
-    first = first.reshape(2, COLS, 2 * SL)
-    base = np.stack([first.real, first.imag], axis=1).reshape(4 * COLS, 2 * SL)
+    bases = []
+    lanes = np.arange(SL) - SL // 2
+    for parity in range(2):
+        c = np.arange(parity, SG, 2)
+        n = np.arange(SL)
+        d = np.exp(2j * np.pi * ((c[None, :] * n[:, None]) % SL) / SL).sum(1)
+        d = d / (math.sqrt(SL) * math.sqrt(SG))
+        first = np.stack([d[(16 * col - lanes) % SL] for col in range(2 * COLS)])
+        first = first.reshape(2, COLS, SL)
+        bases.append(np.stack([first.real, first.imag], axis=1).reshape(4 * COLS, SL))
+    base = np.stack(bases)
 
     k1 = np.arange(K1)
     f = np.arange(NF)
@@ -108,14 +111,13 @@
     raw, table, base_v, win_v, over_facets_v, twiddle_v, over_rows_v, order_v, slots_v,
     slot_s, offset_s, pos_v,
     send1, recv1, send2,
-    raw_sem, const_sem, own_sem, send1_sem, recv1_sem, send2_sem, recv2_sem, send3_sem, recv3_sem,
+    raw_sem, const_sem, own_sem, send1_sem, recv1_sem, send2_sem, recv2_sem, ready,
 ):
     me = lax.axis_index("facet")
     band = lax.axis_index("band")
     x = me // (NY * NC)
     y = (me // NC) % NY
     core = me % NC
-
     rows_of = [lax.rem(x + dx, NX) * (NY * NC) for dx in range(NX)]
     places = [lax.rem(y + dy, NY) * NC for dy in range(NY)]
     cores = [core, 1 - core]
@@ -136,52 +138,64 @@
         )
     ]
     consts[0].start()
-    quarter = SL // 4
+    eighth = SL // 8
     loads = [
         pltpu.make_async_copy(
-            facets.at[:, :, pl.ds(quarter * i, quarter)],
-            raw.at[:, :, pl.ds(quarter * i, quarter)],
+            facets.at[:, :, pl.ds(eighth * i, eighth)],
+            raw.at[:, :, pl.ds(eighth * i, eighth)],
             raw_sem.at[i],
         )
-        for i in range(4)
+        for i in range(8)
     ]
     consts[1].start()
-    for copy in loads:
-        copy.start()
+    for i in (0, 4, 1, 5, 2, 6, 3, 7):
+        loads[i].start()
 
     barrier = pltpu.get_barrier_semaphore()
-    each_peer(
-        lambda dx, p: pl.semaphore_signal(
-            barrier, inc=1, device_id=(band, p), device_id_type=MESH
-        )
-    )
+
+    def signal(to_band, to):
+        pl.semaphore_signal(barrier, inc=1, device_id=(to_band, to), device_id_type=MESH)
+
+    each_peer(lambda dx, p: signal(band, p))
     for i in range(1, NB):
-        pl.semaphore_signal(
-            barrier, inc=1, device_id=(lax.rem(band + i, NB), me), device_id_type=MESH
-        )
+        signal(lax.rem(band + i, NB), me)
+
     for copy in consts[2:]:
         copy.start()
 
     consts[0].wait()
-    for a in range(SG // (2 * COLS)):
-        table[16 * a : 16 * (a + 1), :] = base_v[:, SL - 128 * a : 2 * SL - 128 * a]
+    mid = SL // 2
+    for a in range(SG // (4 * COLS)):
+        for parity in range(2):
+            table[parity, 16 * a : 16 * (a + 1), :] = base_v[
+                parity, :, mid - 128 * a : 2 * mid - 128 * a
+            ]
 
     consts[1].wait()
-    total = None
+    totals = [None, None]
     for i in range(4):
-        loads[i].wait()
-        cut = pl.ds(quarter * i, quarter)
-        windowed = (raw[:, :, cut].astype(F32) * win_v[:, cut][None]).astype(BF)
-        windowed = windowed.reshape(2 * SR, quarter)
-        product = lax.dot_general(
-            table[:, cut], windowed, (((1,), (1,)), ((), ())), preferred_element_type=F32
-        )
-        total = product if total is None else total + product
-    from_real = total[:, :SR].reshape(NF, 2 * COLS, SR)
-    from_imag = total[:, SR:].reshape(NF, 2 * COLS, SR)
-    swapped = pltpu.roll(from_imag, COLS, 1)
-    part = lax.broadcasted_iota(jnp.int32, swapped.shape, 1)
-    send1[...] = (from_real + jnp.where(part < COLS, -swapped, swapped)).astype(BF)
+        halves = []
+        for j in (i, i + 4):
+            loads[j].wait()
+            cut = pl.ds(eighth * j, eighth)
+            halves.append(raw[:, :, cut].astype(F32) * win_v[:, cut][None])
+        for parity in range(2):
+            mixed = halves[0] - halves[1] if parity else halves[0] + halves[1]
+            mixed = mixed.astype(BF).reshape(2 * SR, eighth)
+            product = lax.dot_general(
+                table[parity, :, eighth * i : eighth * (i + 1)], mixed,
+                (((1,), (1,)), ((), ())), preferred_element_type=F32,
+            )
+            totals[parity] = product if i == 0 else totals[parity] + product
+    part = lax.broadcasted_iota(jnp.int32, (NF // 2, 2 * COLS, SR), 1)
+    for upper in range(2):
+        total = totals[0] - totals[1] if upper else totals[0] + totals[1]
+        from_real = total[:, :SR].reshape(NF // 2, 2 * COLS, SR)
+        from_imag = total[:, SR:].reshape(NF // 2, 2 * COLS, SR)
+        swapped = pltpu.roll(from_imag, COLS, 1)
+        send1[upper * (NF // 2) : (upper + 1) * (NF // 2)] = (
+            from_real + jnp.where(part < COLS, -swapped, swapped)
+        ).astype(BF)
 
     pl.semaphore_wait(barrier, NF - 1 + NB - 1)
 
@@ -193,6 +207,10 @@
     )
     own1 = pltpu.make_async_copy(send1.at[me], recv1.at[me], own_sem.at[0])
     own1.start()
+    for i in range(1, NB):
+        pl.semaphore_signal(
+            ready, inc=1, device_id=(lax.rem(band + i, NB), me), device_id_type=MESH
+        )
 
     for copy in consts[2:]:
         copy.wait()
@@ -230,19 +248,14 @@
     tr, ti = twiddle_v[0], twiddle_v[1]
     zr = (yr * tr - yi * ti).astype(BF)
     zi = (yi * tr + yr * ti).astype(BF)
-    turned = jnp.concatenate(
-        [
-            piece
-            for h in range(KH)
-            for piece in (
-                jnp.concatenate([zr[h * BLOCK : (h + 1) * BLOCK], -zi[h * BLOCK : (h + 1) * BLOCK]], 1),
-                jnp.concatenate([zi[h * BLOCK : (h + 1) * BLOCK], zr[h * BLOCK : (h + 1) * BLOCK]], 1),
-            )
-        ],
-        axis=0,
-    )
+    turned = []
+    for h in range(KH):
+        cut = slice(h * BLOCK, (h + 1) * BLOCK)
+        turned.append(jnp.concatenate([zr[cut], -zi[cut]], 1))
+        turned.append(jnp.concatenate([zi[cut], zr[cut]], 1))
     grid = lax.dot_general(
-        over_rows_v[...], turned, (((1,), (1,)), ((), ())), preferred_element_type=F32
+        over_rows_v[...], jnp.concatenate(turned, 0),
+        (((1,), (1,)), ((), ())), preferred_element_type=F32,
     )
     by_subgrid = jnp.concatenate(
         [grid[:, 2 * BLOCK * h : 2 * BLOCK * (h + 1)] for h in range(KH)], axis=0
@@ -250,27 +263,30 @@
     by_slot = jnp.dot(choose, by_subgrid, preferred_element_type=F32)
     send2[...] = by_slot.reshape(NF, 2, 2 * BLOCK).astype(BF)
 
-    each_peer(
-        lambda dx, p: pltpu.make_async_remote_copy(
-            send2.at[p], held.at[band, me], send2_sem, recv2_sem.at[dx],
-            device_id=(band, p), device_id_type=MESH,
-        ).start()
-    )
+    pl.semaphore_wait(ready, NB - 1)
+
+    def send_slots(to_band, carry):
+        away = (to_band != band).astype(jnp.int32)
+
+        def send(to):
+            pltpu.make_async_remote_copy(
+                send2.at[to], held.at[band, me], send2_sem.at[away], recv2_sem.at[away],
+                device_id=(to_band, to), device_id_type=MESH,
+            ).start()
+
+        each_peer(lambda dx, p: send(p))
+
+        @pl.when(to_band != band)
+        def _():
+            send(me)
+
+        return carry
+
+    lax.fori_loop(0, NB, send_slots, 0)
     own2 = pltpu.make_async_copy(send2.at[me], held.at[band, me], own_sem.at[1])
     own2.start()
     own2.wait()
-    for dx in (0, 1, 3, 2):
-        count = CHUNK if dx else CHUNK - 1
-        wait_for(send2.at[pl.ds(0, count)], recv2_sem.at[dx])
-        piece = pl.ds(pl.multiple_of(lax.rem(x + NX - dx, NX) * CHUNK, CHUNK), CHUNK)
-        for to in range(NB):
-
-            @pl.when(band != to)
-            def _(to=to, piece=piece):
-                pltpu.make_async_remote_copy(
-                    held.at[band, piece], held.at[band, piece], send3_sem, recv3_sem,
-                    device_id=(to, me), device_id_type=MESH,
-                ).start()
+    wait_for(send2.at[pl.ds(0, NF - 1)], recv2_sem.at[0])
 
     own = held[band].astype(F32).reshape(2 * NF, 2 * BLOCK).astype(BF)
     source = lax.broadcasted_iota(jnp.int32, (2 * NF, SG), 0)
@@ -289,10 +305,10 @@
         for p in range(2):
             subgrids[slot, p] = pieces[p].astype(BF)
 
-    wait_for(held.at[pl.ds(0, NB - 1)], recv3_sem)
+    wait_for(held.at[pl.ds(0, NB - 1)], recv2_sem.at[1])
     wait_for(send1.at[pl.ds(0, NF - 1)], send1_sem)
-    wait_for(send2.at[pl.ds(0, NF - 1)], send2_sem)
-    wait_for(held.at[pl.ds(0, NB - 1)], send3_sem)
+    wait_for(send2.at[pl.ds(0, NF - 1)], send2_sem.at[0])
+    wait_for(held.at[pl.ds(0, NB - 1)], send2_sem.at[1])
 
 
 def degrid_kernel(block_band, block_weight, held, pick, col_kernel, row_kernel, own, subgrids, visible):
@@ -358,8 +374,8 @@
         out_specs=(whole,) * 5,
         scratch_shapes=[
             vmem((2, SR, SL), BF),
-            vmem((NF * 2 * COLS, SL), BF),
-            vmem((4 * COLS, 2 * SL), BF),
+            vmem((2, NF * COLS, SL // 2), BF),
+            vmem((2, 4 * COLS, SL), BF),
             vmem((1, SL), F32),
             vmem((2 * HALF, NF * 2 * COLS), BF),
             vmem((2, HALF, SR), F32),
@@ -372,15 +388,14 @@
             vmem((NF, 2 * COLS, SR), BF),
             vmem((NF, 2 * COLS, SR), BF),
             vmem((NF, 2, 2 * BLOCK), BF),
-            dma((4,)),
+            dma((8,)),
             dma((10,)),
             dma((2,)),
             dma,
             dma,
-            dma,
-            dma((NX,)),
-            dma,
-            dma,
+            dma((2,)),
+            dma((2,)),
+            pltpu.SemaphoreType.REGULAR,
         ],
         compiler_params=pltpu.CompilerParams(
             collective_id=0, has_side_effects=True, vmem_limit_bytes=24 * 2**20

time: 39 us -> 35.6 us (0.913)
  Pallas kernels: 38.2 us -> 34.8 us
    pallas_call x1, Pallas kernels: 36.1 us -> 32.7 us  [local(): pl.pallas_call(exchange_kernel, out_shape=(vmem((NB, NF, 2, 2 * BLOCK), B...]
where the time goes in v3:
time: 35.6 us; the launch traced here: 35.4 us
  Pallas kernels  34.8 us (98%)
  between operations  0.67 us (2%)
    pallas_call x1, Pallas kernels, local(): pl.pallas_call(exchange_kernel, out_shape=(vmem((NB, NF, 2, 2 * BLOCK), B...  32.7 us
    pallas_call x1, Pallas kernels, local(): pl.pallas_call(degrid_kernel, out_shape=(jax.ShapeDtypeStruct((2, 2, CR,...  2.08 us

profile of v3, /device:TPU:1, one launch (start us, length us, event | category | flops | bytes accessed | tf_op | source)
XLA Modules:
  0.0 35.4 jit_solution(12399501462046542825)
XLA Ops:
  0.6 0.0 copy-start.1
  0.6 0.0 copy-start
  0.7 32.7 %column_pass.1 = (bf16[8,64,2,128]{3,2,1,0:T(2,128)(2,1)S(1)}, bf16[4,128,512]{2,1,0:T(8,128)(2,1)S(1)}, bf16[2,256,2048]{2,1,0:T(8,128)(2,1)S(1)}, f32[4,16,204...) custom-call(bf16[2,128,4096]{2,1,0:T(8,128)(2,1)} %bitcast.6, f32[1,4096]{1,0:T(1,128)} %bitcast.8, ...), custom_call_target="tpu_custom_call" | custom-call | tf_op jit(solution)/shard_map/column_pass/pallas_call | solution.py:364
  33.3 0.0 copy-done.1
  33.3 0.0 copy-done
  33.4 2.1 %degrid.1 = (bf16[2,2,16,256]{3,2,1,0:T(8,128)(2,1)}, f32[4,2,2048]{2,1,0:T(2,128)}) custom-call(s32[1,1,4]{2,1,0:T(1,128)S(1)} %copy-done, f32[1,1,4]{2,1,0:T(1,128)S(1)} %copy-done.1, bf16[8,64,2,128]{3,2,1,0:T(2,128)(2,1)S(1)} %get-tuple-element.9.held, bf16[4,128,512]{2,1,0:T(8,128)(2,1)S(1)} %get-tuple-element.10.pick, ...), custom_call_target="tpu_custom_call" | custom-call | tf_op jit(solution)/shard_map/degrid/pallas_call | solution.py:406
Async XLA Ops:
  0.6 32.7 %copy-start.1 = (f32[1,1,4]{2,1,0:T(1,128)S(1)}, f32[1,1,4]{2,1,0:T(1,128)}, u32[]{:S(2)}) copy-start(f32[1,1,4]{2,1,0:T(1,128)} %block_weight.1) | copy-start | bytes 52
  0.6 32.7 %copy-start = (s32[1,1,4]{2,1,0:T(1,128)S(1)}, s32[1,1,4]{2,1,0:T(1,128)}, u32[]{:S(2)}) copy-start(s32[1,1,4]{2,1,0:T(1,128)} %block_band.1) | copy-start | bytes 52

commit v4 on v3

--- a/solution.py
+++ b/solution.py
@@ -106,11 +106,11 @@
 
 def exchange_kernel(
     facets, window, base, over_facets, twiddle, over_rows, order, slots,
-    block_slot, block_offset, vis_pos,
-    held, pick, col_kernel, row_kernel, subgrids,
+    block_slot, block_band, block_offset, block_weight, vis_pos,
+    left, col_kernel, row_kernel, subgrids,
     raw, table, base_v, win_v, over_facets_v, twiddle_v, over_rows_v, order_v, slots_v,
-    slot_s, offset_s, pos_v,
-    send1, recv1, send2,
+    slot_s, band_s, offset_s, weight_s, pos_v,
+    send1, recv1, send2, held, pick,
     raw_sem, const_sem, own_sem, send1_sem, recv1_sem, send2_sem, recv2_sem, ready,
 ):
     me = lax.axis_index("facet")
@@ -132,8 +132,8 @@
             (
                 (base, base_v), (window, win_v), (over_facets, over_facets_v),
                 (twiddle, twiddle_v), (over_rows, over_rows_v), (order, order_v),
-                (slots, slots_v), (block_slot, slot_s), (block_offset, offset_s),
-                (vis_pos, pos_v),
+                (slots, slots_v), (block_slot, slot_s), (block_band, band_s),
+                (block_offset, offset_s), (block_weight, weight_s), (vis_pos, pos_v),
             )
         )
     ]
@@ -306,38 +306,45 @@
             subgrids[slot, p] = pieces[p].astype(BF)
 
     wait_for(held.at[pl.ds(0, NB - 1)], recv2_sem.at[1])
-    wait_for(send1.at[pl.ds(0, NF - 1)], send1_sem)
-    wait_for(send2.at[pl.ds(0, NF - 1)], send2_sem.at[0])
-    wait_for(held.at[pl.ds(0, NB - 1)], send2_sem.at[1])
-
-
-def degrid_kernel(block_band, block_weight, held, pick, col_kernel, row_kernel, own, subgrids, visible):
-    subgrids[...] = own[...]
     nothing = jnp.zeros((2 * CR, PC), BF)
     for pair in range(VB // 2):
         patches = []
         for v in (2 * pair, 2 * pair + 1):
-            lo = block_band[0, 0, v]
-            weight = block_weight[0, 0, v]
+            lo = band_s[0, 0, v]
+            weight = weight_s[0, 0, v]
             mixed = (1.0 - weight) * held[lo].astype(F32) + weight * held[lo + 1].astype(F32)
             mixed = mixed.reshape(2 * NF, 2 * BLOCK).astype(BF)
             pieces = joined(spread(mixed, pick[v]), PC)
             patches.append(jnp.concatenate(pieces, axis=0).astype(BF))
-        left = jnp.concatenate(
+        left[pair] = jnp.concatenate(
             [
                 jnp.concatenate([patches[0], nothing], 1),
                 jnp.concatenate([nothing, patches[1]], 1),
             ],
             axis=0,
         )
-        summed = jnp.dot(left, col_kernel[pair], preferred_element_type=F32)
+    wait_for(send1.at[pl.ds(0, NF - 1)], send1_sem)
+    wait_for(send2.at[pl.ds(0, NF - 1)], send2_sem.at[0])
+    wait_for(held.at[pl.ds(0, NB - 1)], send2_sem.at[1])
+
+
+def degrid_kernel(left, col_kernel, row_kernel, own, subgrids, visible, made, sems):
+    outs = [pltpu.make_async_copy(own, subgrids, sems.at[0])]
+    outs[0].start()
+    for pair in range(VB // 2):
+        summed = jnp.dot(left[pair], col_kernel[pair], preferred_element_type=F32)
         for b in range(2):
             v = 2 * pair + b
             for p in range(2):
                 at = (2 * b + p) * CR
-                visible[v, p : p + 1, :] = jnp.sum(
+                made[v, p : p + 1, :] = jnp.sum(
                     summed[at : at + CR] * row_kernel[v], axis=0, keepdims=True
                 )
+        part = pl.ds(2 * pair, 2)
+        outs.append(pltpu.make_async_copy(made.at[part], visible.at[part], sems.at[1 + pair]))
+        outs[-1].start()
+    for copy in outs:
+        copy.wait()
 
 
 def local(
@@ -358,20 +365,21 @@
         jnp.asarray(order, BF),
         slot_of_subgrid[None],
         block_slot,
+        block_band,
         block_offset,
+        block_weight,
         vis_pos[0, 0],
     )
     made = pl.pallas_call(
         exchange_kernel,
         out_shape=(
-            vmem((NB, NF, 2, 2 * BLOCK), BF),
-            vmem((VB, 2 * NF, COLS * PC), BF),
+            vmem((VB // 2, 4 * CR, 2 * PC), BF),
             vmem((VB // 2, 2 * PC, NV), BF),
             vmem((VB, CR, NV), F32),
             vmem((2, 2, CR, SG), BF),
         ),
         in_specs=[anywhere] * len(args),
-        out_specs=(whole,) * 5,
+        out_specs=(whole,) * 4,
         scratch_shapes=[
             vmem((2, SR, SL), BF),
             vmem((2, NF * COLS, SL // 2), BF),
@@ -384,12 +392,16 @@
             vmem((1, NS), jnp.int32),
             pltpu.SMEM((1, 1, VB), jnp.int32),
             pltpu.SMEM((1, 1, VB), jnp.int32),
+            pltpu.SMEM((1, 1, VB), jnp.int32),
+            pltpu.SMEM((1, 1, VB), F32),
             vmem((VB, 2, NV), F32),
             vmem((NF, 2 * COLS, SR), BF),
             vmem((NF, 2 * COLS, SR), BF),
             vmem((NF, 2, 2 * BLOCK), BF),
+            vmem((NB, NF, 2, 2 * BLOCK), BF),
+            vmem((VB, 2 * NF, COLS * PC), BF),
             dma((8,)),
-            dma((10,)),
+            dma((12,)),
             dma((2,)),
             dma,
             dma,
@@ -402,18 +414,18 @@
         ),
         name="column_pass",
     )(*(pltpu.with_memory_space_constraint(a, pltpu.HBM) for a in args))
-    scalars = pl.BlockSpec(memory_space=pltpu.SMEM)
     subgrids, visible = pl.pallas_call(
         degrid_kernel,
         out_shape=(
             jax.ShapeDtypeStruct((2, 2, CR, SG), BF),
             jax.ShapeDtypeStruct((VB, 2, NV), F32),
         ),
-        in_specs=[scalars, scalars] + [whole] * 5,
-        out_specs=(whole, whole),
+        in_specs=[whole] * 4,
+        out_specs=(anywhere, anywhere),
+        scratch_shapes=[vmem((VB, 2, NV), F32), dma((3,))],
         compiler_params=pltpu.CompilerParams(vmem_limit_bytes=24 * 2**20),
         name="degrid",
-    )(block_band, block_weight, *made)
+    )(*made)
     return subgrids[None], visible[None, None]
 
 

time: 35.6 us -> 34.9 us (0.980)
  Pallas kernels: 34.8 us -> 34.2 us
    pallas_call x1, Pallas kernels: 2.08 us -> 1.16 us  [local(): pl.pallas_call(degrid_kernel, out_shape=(jax.ShapeDtypeStruct((2, 2, CR,...]
where the time goes in v4:
time: 34.9 us; the launch traced here: 34.8 us
  Pallas kernels  34.2 us (98%)
  between operations  0.64 us (2%)
    pallas_call x1, Pallas kernels, local(): pl.pallas_call(exchange_kernel, out_shape=(vmem((VB // 2, 4 * CR, 2 * PC)...  33 us
    pallas_call x1, Pallas kernels, local(): pl.pallas_call(degrid_kernel, out_shape=(jax.ShapeDtypeStruct((2, 2, CR,...  1.16 us

profile of v4, /device:TPU:1, one launch (start us, length us, event | category | flops | bytes accessed | tf_op | source)
XLA Modules:
  0.0 34.8 jit_solution(1181186938441787198)
XLA Ops:
  0.6 33.0 %column_pass.1 = (bf16[2,64,256]{2,1,0:T(8,128)(2,1)S(1)}, bf16[2,256,2048]{2,1,0:T(8,128)(2,1)S(1)}, f32[4,16,2048]{2,1,0:T(8,128)S(1)}, bf16[2,2,16,256]{3,2,1,0:T(8,128)(2,1)S(1)}) custom-call(bf16[2,128,4096]{2,1,0:T(8,128)(2,1)} %bitcast.6, f32[1,4096]{1,0:T(1,128)} %bitcast.8, bf16[2,16,4096]{2,1,0:T(8,128)(2,1)} %constant.10.clone.base, ...), custom_call_target="tpu_custom_call" | custom-call | tf_op jit(solution)/shard_map/column_pass/pallas_call | solution.py:373
  33.6 1.2 %degrid.1 = (bf16[2,2,16,256]{3,2,1,0:T(8,128)(2,1)}, f32[4,2,2048]{2,1,0:T(2,128)}) custom-call(bf16[2,64,256]{2,1,0:T(8,128)(2,1)S(1)} %get-tuple-element.8.left, bf16[2,256,2048]{2,1,0:T(8,128)(2,1)S(1)} %get-tuple-element.9.col_kernel, f32[4,16,2048]{2,1,0:T(8,128)S(1)} %get-tuple-element.10.row_kernel, bf16[2,2,16,256]{3,2,1,0:T(8,128)(2,1)S(1)} %get-tuple-element.11.own), custom_call_target="tpu_custom_call" | custom-call | tf_op jit(solution)/shard_map/degrid/pallas_call | solution.py:417

commit v5 on v4

--- a/solution.py
+++ b/solution.py
@@ -41,6 +41,9 @@
     ),
     key=lambda t: -(4 * min(t[0], NX - t[0]) + 4 * min(t[1], NY - t[1]) + t[2]),
 )
+FIRST = sorted(
+    range(NF), key=lambda f: 2 * min(f // NC % NY, NY - f // NC % NY) + f // (NY * NC)
+)
 
 
 def tables():
@@ -81,7 +84,11 @@
     order = np.zeros((NS, KH * K2))
     for s in range(NS):
         order[s, (s % KH) * K2 + s // KH] = 1.0
-    return base, over_facets, twiddle, over_rows, order
+    packed = np.zeros((2 * HALF + K2 + NS, NF * 2 * COLS))
+    packed[: 2 * HALF] = over_facets
+    packed[2 * HALF : 2 * HALF + K2, : 2 * SR] = over_rows
+    packed[2 * HALF + K2 :, : KH * K2] = order
+    return base, packed, twiddle
 
 
 def wait_for(ref, sem):
@@ -105,10 +112,10 @@
 
 
 def exchange_kernel(
-    facets, window, base, over_facets, twiddle, over_rows, order, slots,
+    facets, window, base, packed, twiddle, slots,
     block_slot, block_band, block_offset, block_weight, vis_pos,
     left, col_kernel, row_kernel, subgrids,
-    raw, table, base_v, win_v, over_facets_v, twiddle_v, over_rows_v, order_v, slots_v,
+    raw, table, base_v, win_v, packed_v, twiddle_v, slots_v,
     slot_s, band_s, offset_s, weight_s, pos_v,
     send1, recv1, send2, held, pick,
     raw_sem, const_sem, own_sem, send1_sem, recv1_sem, send2_sem, recv2_sem, ready,
@@ -126,30 +133,29 @@
         for dx, dy, dc in PEERS:
             do(dx, rows_of[dx] + places[dy] + cores[dc])
 
+    early_consts = [
+        pltpu.make_async_copy(base, base_v, send1_sem),
+        pltpu.make_async_copy(window, win_v, own_sem),
+    ]
     consts = [
-        pltpu.make_async_copy(src, dst, const_sem.at[i])
-        for i, (src, dst) in enumerate(
-            (
-                (base, base_v), (window, win_v), (over_facets, over_facets_v),
-                (twiddle, twiddle_v), (over_rows, over_rows_v), (order, order_v),
-                (slots, slots_v), (block_slot, slot_s), (block_band, band_s),
-                (block_offset, offset_s), (block_weight, weight_s), (vis_pos, pos_v),
-            )
-        )
+        pltpu.make_async_copy(packed, packed_v, send2_sem.at[0]),
+        pltpu.make_async_copy(twiddle, twiddle_v, send2_sem.at[1]),
+        pltpu.make_async_copy(slots, slots_v, const_sem.at[0]),
+        pltpu.make_async_copy(vis_pos, pos_v, const_sem.at[1]),
     ]
-    consts[0].start()
-    eighth = SL // 8
-    loads = [
-        pltpu.make_async_copy(
-            facets.at[:, :, pl.ds(eighth * i, eighth)],
-            raw.at[:, :, pl.ds(eighth * i, eighth)],
-            raw_sem.at[i],
-        )
-        for i in range(8)
+    scalars = [
+        pltpu.make_async_copy(block_slot, slot_s, raw_sem.at[0]),
+        pltpu.make_async_copy(block_offset, offset_s, raw_sem.at[1]),
+        pltpu.make_async_copy(block_band, band_s, raw_sem.at[0]),
+        pltpu.make_async_copy(block_weight, weight_s, raw_sem.at[1]),
     ]
-    consts[1].start()
-    for i in (0, 4, 1, 5, 2, 6, 3, 7):
-        loads[i].start()
+    early_consts[0].start()
+    early_consts[1].start()
+    quarter, eighth = SL // 4, SL // 8
+    for i in range(2):
+        for j in (i, i + 2):
+            cut = pl.ds(quarter * j, quarter)
+            pltpu.make_async_copy(facets.at[:, :, cut], raw.at[:, :, cut], raw_sem.at[i]).start()
 
     barrier = pltpu.get_barrier_semaphore()
 
@@ -160,10 +166,10 @@
     for i in range(1, NB):
         signal(lax.rem(band + i, NB), me)
 
-    for copy in consts[2:]:
+    for copy in consts:
         copy.start()
 
-    consts[0].wait()
+    early_consts[0].wait()
     mid = SL // 2
     for a in range(SG // (4 * COLS)):
         for parity in range(2):
@@ -171,12 +177,13 @@
                 parity, :, mid - 128 * a : 2 * mid - 128 * a
             ]
 
-    consts[1].wait()
+    early_consts[1].wait()
     totals = [None, None]
     for i in range(4):
         halves = []
+        if i % 2 == 0:
+            wait_for(raw.at[:, :, pl.ds(0, 2 * quarter)], raw_sem.at[i // 2])
         for j in (i, i + 4):
-            loads[j].wait()
             cut = pl.ds(eighth * j, eighth)
             halves.append(raw[:, :, cut].astype(F32) * win_v[:, cut][None])
         for parity in range(2):
@@ -197,26 +204,30 @@
             from_real + jnp.where(part < COLS, -swapped, swapped)
         ).astype(BF)
 
+    scalars[0].start()
+    scalars[1].start()
     pl.semaphore_wait(barrier, NF - 1 + NB - 1)
 
     each_peer(
         lambda dx, p: pltpu.make_async_remote_copy(
-            send1.at[p], recv1.at[me], send1_sem, recv1_sem,
+            send1.at[p], recv1.at[me], send1_sem, recv1_sem.at[dx],
             device_id=(band, p), device_id_type=MESH,
         ).start()
     )
-    own1 = pltpu.make_async_copy(send1.at[me], recv1.at[me], own_sem.at[0])
+    own1 = pltpu.make_async_copy(send1.at[me], recv1.at[me], own_sem)
     own1.start()
     for i in range(1, NB):
         pl.semaphore_signal(
             ready, inc=1, device_id=(lax.rem(band + i, NB), me), device_id_type=MESH
         )
 
-    for copy in consts[2:]:
+    for copy in consts + scalars[:2]:
         copy.wait()
+    scalars[2].start()
+    scalars[3].start()
     named = lax.broadcasted_iota(jnp.int32, (2 * NF, NS), 0) == slots_v[...]
     choose = jnp.dot(
-        jnp.where(named, 1.0, 0.0).astype(BF), order_v[...], preferred_element_type=F32
+        jnp.where(named, 1.0, 0.0).astype(BF), packed_v[2 * HALF + K2 :, : KH * K2], preferred_element_type=F32
     ).astype(BF)
     scale = 1.0 / (2.0 * SIGMA * SIGMA)
     rows = lax.broadcasted_iota(jnp.int32, (CR, NV), 0).astype(F32)
@@ -240,10 +251,21 @@
             )
             pick[v, :, pl.ds(PC * c, PC)] = jnp.where(hit, 1.0, 0.0).astype(BF)
 
+    scalars[2].wait()
+    scalars[3].wait()
+
     own1.wait()
-    wait_for(recv1.at[pl.ds(0, NF - 1)], recv1_sem)
-    arrived = recv1[...].astype(F32).reshape(NF * 2 * COLS, SR).astype(BF)
-    over = jnp.dot(over_facets_v[...], arrived, preferred_element_type=F32)
+    over = None
+    for dx in (0, 1, 3, 2):
+        count = CHUNK if dx else CHUNK - 1
+        row = pl.multiple_of(lax.rem(x + NX - dx, NX) * CHUNK, CHUNK)
+        wait_for(recv1.at[pl.ds(0, count)], recv1_sem.at[dx])
+        arrived = recv1[pl.ds(row, CHUNK)].astype(F32).reshape(CHUNK * 2 * COLS, SR).astype(BF)
+        lanes = pl.ds(pl.multiple_of(row * 2 * COLS, CHUNK * 2 * COLS), CHUNK * 2 * COLS)
+        product = jnp.dot(
+            packed_v[: 2 * HALF, lanes], arrived, preferred_element_type=F32
+        )
+        over = product if over is None else over + product
     yr, yi = over[:HALF], over[HALF:]
     tr, ti = twiddle_v[0], twiddle_v[1]
     zr = (yr * tr - yi * ti).astype(BF)
@@ -254,7 +276,7 @@
         turned.append(jnp.concatenate([zr[cut], -zi[cut]], 1))
         turned.append(jnp.concatenate([zi[cut], zr[cut]], 1))
     grid = lax.dot_general(
-        over_rows_v[...], jnp.concatenate(turned, 0),
+        packed_v[2 * HALF : 2 * HALF + K2, : 2 * SR], jnp.concatenate(turned, 0),
         (((1,), (1,)), ((), ())), preferred_element_type=F32,
     )
     by_subgrid = jnp.concatenate(
@@ -274,16 +296,19 @@
                 device_id=(to_band, to), device_id_type=MESH,
             ).start()
 
-        each_peer(lambda dx, p: send(p))
+        @pl.when(to_band == band)
+        def _():
+            each_peer(lambda dx, p: send(p))
 
         @pl.when(to_band != band)
         def _():
-            send(me)
+            for to in FIRST:
+                send(to)
 
         return carry
 
     lax.fori_loop(0, NB, send_slots, 0)
-    own2 = pltpu.make_async_copy(send2.at[me], held.at[band, me], own_sem.at[1])
+    own2 = pltpu.make_async_copy(send2.at[me], held.at[band, me], own_sem)
     own2.start()
     own2.wait()
     wait_for(send2.at[pl.ds(0, NF - 1)], recv2_sem.at[0])
@@ -350,7 +375,7 @@
 def local(
     facets, col_window, slot_of_subgrid, block_slot, block_band, block_offset, block_weight, vis_pos
 ):
-    base, over_facets, twiddle, over_rows, order = tables()
+    base, packed, twiddle = tables()
     anywhere = pl.BlockSpec(memory_space=pltpu.HBM)
     whole = pl.BlockSpec(memory_space=pltpu.VMEM)
     dma = pltpu.SemaphoreType.DMA
@@ -359,10 +384,8 @@
         facets[0, 0],
         col_window[None],
         jnp.asarray(base, BF),
-        jnp.asarray(over_facets, BF),
+        jnp.asarray(packed, BF),
         jnp.asarray(twiddle, F32),
-        jnp.asarray(over_rows, BF),
-        jnp.asarray(order, BF),
         slot_of_subgrid[None],
         block_slot,
         block_band,
@@ -385,10 +408,8 @@
             vmem((2, NF * COLS, SL // 2), BF),
             vmem((2, 4 * COLS, SL), BF),
             vmem((1, SL), F32),
-            vmem((2 * HALF, NF * 2 * COLS), BF),
+            vmem((2 * HALF + K2 + NS, NF * 2 * COLS), BF),
             vmem((2, HALF, SR), F32),
-            vmem((K2, 2 * SR), BF),
-            vmem((NS, KH * K2), BF),
             vmem((1, NS), jnp.int32),
             pltpu.SMEM((1, 1, VB), jnp.int32),
             pltpu.SMEM((1, 1, VB), jnp.int32),
@@ -400,11 +421,11 @@
             vmem((NF, 2, 2 * BLOCK), BF),
             vmem((NB, NF, 2, 2 * BLOCK), BF),
             vmem((VB, 2 * NF, COLS * PC), BF),
-            dma((8,)),
-            dma((12,)),
+            dma((2,)),
             dma((2,)),
             dma,
             dma,
+            dma((NX,)),
             dma((2,)),
             dma((2,)),
             pltpu.SemaphoreType.REGULAR,

time: 34.9 us -> 34.7 us (level)
  no operation moved by 1% of the time
where the time goes in v5:
time: 34.7 us; the launch traced here: 34.5 us
  Pallas kernels  33.9 us (98%)
  between operations  0.64 us (2%)
    pallas_call x1, Pallas kernels, local(): pl.pallas_call(exchange_kernel, out_shape=(vmem((VB // 2, 4 * CR, 2 * PC)...  32.7 us
    pallas_call x1, Pallas kernels, local(): pl.pallas_call(degrid_kernel, out_shape=(jax.ShapeDtypeStruct((2, 2, CR,...  1.16 us

profile of v5, /device:TPU:1, one launch (start us, length us, event | category | flops | bytes accessed | tf_op | source)
XLA Modules:
  0.0 34.5 jit_solution(8530762748884191697)
XLA Ops:
  0.6 32.7 %column_pass.1 = (bf16[2,64,256]{2,1,0:T(8,128)(2,1)S(1)}, bf16[2,256,2048]{2,1,0:T(8,128)(2,1)S(1)}, f32[4,16,2048]{2,1,0:T(8,128)S(1)}, bf16[2,2,16,256]{3,2,1,0:T(8,128)(2,1)S(1)}) custom-call(bf16[2,128,4096]{2,1,0:T(8,128)(2,1)} %bitcast.6, f32[1,4096]{1,0:T(1,128)} %bitcast.8, bf16[2,16,4096]{2,1,0:T(8,128)(2,1)} %constant.6.clone.base, ...), custom_call_target="tpu_custom_call" | custom-call | tf_op jit(solution)/shard_map/column_pass/pallas_call | solution.py:396
  33.4 1.2 %degrid.1 = (bf16[2,2,16,256]{3,2,1,0:T(8,128)(2,1)}, f32[4,2,2048]{2,1,0:T(2,128)}) custom-call(bf16[2,64,256]{2,1,0:T(8,128)(2,1)S(1)} %get-tuple-element.8.left, bf16[2,256,2048]{2,1,0:T(8,128)(2,1)S(1)} %get-tuple-element.9.col_kernel, f32[4,16,2048]{2,1,0:T(8,128)S(1)} %get-tuple-element.10.row_kernel, bf16[2,2,16,256]{3,2,1,0:T(8,128)(2,1)S(1)} %get-tuple-element.11.own), custom_call_target="tpu_custom_call" | custom-call | tf_op jit(solution)/shard_map/degrid/pallas_call | solution.py:438
